TPU v7x, 32 devices: a whole 2x2x4 slice. The times are simulated.
32 devices in a mesh: op: 16 (over z, x, core), sec: 2 (over y).
Axes of the slice: x: 2, y: 2, z: 4, core: 2. Of those that a mesh axis runs over, the one named last changes fastest.
Arguments:
- left_ops: float32 [16, 2, 1024, 1024], P('op', 'sec'), may hold values from -0.5 to 3.5
- right_ops: float32 [16, 2, 1024, 1024], P('op', 'sec'), may hold values from -0.5 to 3.5
- amplitudes: float32 [2, 1024, 1024], P('sec', 'op'), may hold values from -72 to 72
- sketch: float32 [1024, 512], replicated, may hold values from -0.1875 to 0.1875
- sector_shift: int32 [16], P('op'), may hold values from 0 to 3
Outputs:
- rotated: float32 [16, 2, 512, 512], P('op', 'sec')
- new_basis: float32 [2, 1024, 512], P('sec', 'op')
- energy: float32 [], replicated
Inputs may be any that keep to these rules, and one draw needn't show every extreme that they name: The target sector of pair k from source sector s is (s + sector_shift[k]) mod 2.
All inputs are finite; a program needn't handle non-finite values.
Results may differ from a plain program's by a relative error of at most 0.0003.
Values sent between devices are 32-bit elements; how exact they have to be, the bound alone decides.
A program may use at most 128 MiB of HBM per device.

v0:
```python
import jax
import jax.numpy as jnp
from jax import lax
from jax.sharding import PartitionSpec as P

EXACT = lax.Precision.HIGHEST


def shifted_2(block, axis, distance):
    devices = range(lax.axis_size(axis))
    route = [((i - distance) % len(devices), i) for i in devices]
    return lax.ppermute(block, axis, route)


def matmul(first, second):
    return jnp.dot(first, second, precision=EXACT, preferred_element_type=jnp.float32)


def contract_rows(first, second):
    return jnp.einsum("rk,rl->kl", first, second, precision=EXACT)


def body(left_ops, right_ops, amplitudes, sketch, sector_shift):
    left_op = left_ops[0, 0]
    right_op = right_ops[0, 0]
    state_slab = amplitudes[0]
    offset = sector_shift[0]
    right_part = matmul(lax.all_gather(state_slab, "op", axis=0, tiled=True), right_op)
    term_full = matmul(left_op, right_part)
    shifted = term_full
    for bit_index in range(2):
        arrived = shifted_2(shifted, "sec", 1 << bit_index)
        chosen = offset >> bit_index & 1 == 1
        shifted = jnp.where(chosen, arrived, shifted)
    product_slab = lax.psum_scatter(shifted, "op", scatter_dimension=0, tiled=True)
    correlation = jnp.sum(state_slab * product_slab)
    norm_sq = jnp.sum(state_slab * state_slab)
    first_sk = matmul(product_slab, sketch)
    second_sk = matmul(state_slab, sketch)
    summed = lax.psum(
        (
            contract_rows(first_sk, first_sk),
            contract_rows(first_sk, second_sk),
            contract_rows(second_sk, second_sk),
            correlation,
            norm_sq,
        ),
        "op",
    )
    totals = lax.psum((summed[3], summed[4]), "sec")
    energy = totals[0] / totals[1]
    cross_mat = summed[1]
    gram_mat = summed[0] - energy * (cross_mat + cross_mat.T) + energy * energy * summed[2]
    sketched = first_sk - energy * second_sk
    factor = jnp.linalg.cholesky(gram_mat)
    basis_slab = jax.scipy.linalg.solve_triangular(factor, sketched.T, lower=True).T
    basis_full = lax.all_gather(basis_slab, "op", axis=0, tiled=True)
    target = basis_full
    for bit_index in range(2):
        arrived = shifted_2(target, "sec", -(1 << bit_index))
        chosen = offset >> bit_index & 1 == 1
        target = jnp.where(chosen, arrived, target)
    applied = matmul(left_op, basis_full)
    rotated = contract_rows(target, applied)
    return (rotated[None, None], basis_slab[None], energy)


def solution(mesh):
    in_specs = (
        P("op", "sec", None, None),
        P("op", "sec", None, None),
        P("sec", "op", None),
        P(),
        P("op"),
    )
    out_specs = (P("op", "sec", None, None), P("sec", "op", None), P())
    return jax.shard_map(body, mesh=mesh, in_specs=in_specs, out_specs=out_specs, check_vma=False)
```

profile of v0, /device:TPU:0, one launch (start us, length us, event | category | flops | bytes accessed | tf_op | source)
XLA Modules:
  0.0 672.1 jit_solution(10956362200664981195)
XLA Ops:
  8.0 55.3 %all-gather.6.cloned.1.call-done = f32[1,1024,1024]{2,1,0:T(8,128)} async-done(((f32[1,64,1024]{2,1,0:T(8,128)}), f32[1,1024,1024]{2,1,0:T(8,128)}) %all-gather.6.cloned.1.call-update) | async-done | bytes 4194320 | tf_op jit(solution)/shard_map/all_gather | solution.py:28
  63.3 17.1 %fusion.4 = f32[1024,1024]{1,0:T(8,128)S(1)} fusion(f32[1,1,1024,1024]{3,2,1,0:T(8,128)} %param.6, f32[1,1024,1024]{2,1,0:T(8,128)} %all-gather.6.cloned.1.call-done), kind=kOutput, calls=%fused_computation.6 | convolution fusion | flops 12884901888 | bytes 12582912 | tf_op jit(solution)/shard_map/dot_general | solution.py:16
  80.4 28.0 %fusion.7 = f32[1024,1024]{0,1:T(8,128)S(1)} fusion(f32[1024,1024]{1,0:T(8,128)S(1)} %fusion.4, f32[1,1,1024,1024]{3,2,1,0:T(8,128)S(1)} %copy-done.2), kind=kOutput, calls=%fused_computation.9 | convolution fusion | flops 12884901888 | bytes 12582912 | tf_op jit(solution)/shard_map/dot_general | solution.py:16
  110.6 90.6 %collective-permute-done = f32[1024,1024]{0,1:T(8,128)S(1)} collective-permute-done((f32[1024,1024]{0,1:T(8,128)S(1)}, f32[1024,1024]{0,1:T(8,128)S(1)}, u32[]{:S(2)}, u32[]{:S(2)}) %collective-permute-start) | collective-permute-done | bytes 4194336 | tf_op jit(solution)/shard_map/ppermute | solution.py:12
  202.8 2.9 broadcast_select_fusion.1
  205.7 5.3 copy.20
  215.4 67.2 %reduce-scatter.4.cloned.1.call-done = f32[64,1024]{1,0:T(8,128)} async-done(((f32[1024,1024]{1,0:T(8,128)}), f32[64,1024]{1,0:T(8,128)}) %reduce-scatter.4.cloned.1.call-update) | async-done | bytes 262160
  282.6 2.4 fusion.56
  285.0 2.0 fusion.58
  292.1 30.9 %all-reduce.1 = (f32[]{:T(128)}, f32[]{:T(128)}) all-reduce(f32[]{:T(128)} %get-tuple-element.12, f32[]{:T(128)} %get-tuple-element.11), channel_id=1, replica_groups=mesh['op'=16,'sec'=2] {'op'}, use_global_device_ids=true, to_apply=%region_3.4 | all-reduce | flops 2 | bytes 16 | tf_op jit(solution)/shard_map/psum | solution.py:40
  323.0 6.0 all-reduce.3
  330.3 62.5 %all-reduce.6.cloned.1.call-done = (f32[512,512]{0,1:T(8,128)}, f32[512,512]{1,0:T(8,128)}, f32[512,512]{0,1:T(8,128)}) async-done(((f32[512,512]{0,1:T(8,128)}, f32[512,512]{1,0:T(8,128)}, f32[512,512]{0,1:T(8,128)}), (f32[512,512]{0,1:T(8,128)}, f32[512,512]{1,0:T(8,128)}, f32[512,512]{0,1:T(8,128)})) %all-reduce.6.cloned.1.call-update) | async-done | bytes 3145744 | tf_op jit(solution)/shard_map/psum | solution.py:40
  392.8 2.5 copy.15
  395.4 2.7 fusion.18
  401.8 11.7 %cholesky.104 = f32[128,128]{1,0:T(8,128)S(1)} custom-call(f32[128,128]{1,0:T(8,128)S(1)} %cholesky.266), custom_call_target="Cholesky" | custom-call | tf_op jit(solution)/shard_map/jit(cholesky)/cholesky | solution.py:55
  413.6 9.8 %custom-call.31 = f32[1,128,128]{1,2,0:T(8,128)S(1)} custom-call(f32[1,128,128]{2,1,0:T(8,128)S(1)} %get-tuple-element.41), custom_call_target="InvertDiagBlocksLowerTriangular" | custom-call | tf_op jit(solution)/shard_map/jit(cholesky)/cholesky | solution.py:55
  426.6 12.5 %cholesky.217 = f32[128,128]{1,0:T(8,128)S(1)} custom-call(f32[128,128]{1,0:T(8,128)} %cholesky.270), custom_call_target="Cholesky" | custom-call | tf_op jit(solution)/shard_map/jit(cholesky)/cholesky | solution.py:55
  439.8 10.8 %custom-call.32 = f32[1,128,128]{1,2,0:T(8,128)S(1)} custom-call(f32[1,128,128]{2,1,0:T(8,128)} %get-tuple-element.38), custom_call_target="InvertDiagBlocksLowerTriangular" | custom-call | tf_op jit(solution)/shard_map/jit(cholesky)/cholesky | solution.py:55
  452.2 11.7 %cholesky.238 = f32[128,128]{1,0:T(8,128)S(1)} custom-call(f32[128,128]{1,0:T(8,128)S(1)} %cholesky.275), custom_call_target="Cholesky" | custom-call | tf_op jit(solution)/shard_map/jit(cholesky)/cholesky | solution.py:55
  464.6 9.8 %custom-call.33 = f32[1,128,128]{1,2,0:T(8,128)S(1)} custom-call(f32[1,128,128]{2,1,0:T(8,128)S(1)} %get-tuple-element.35), custom_call_target="InvertDiagBlocksLowerTriangular" | custom-call | tf_op jit(solution)/shard_map/jit(cholesky)/cholesky | solution.py:55
  475.8 11.9 %cholesky.255 = f32[128,128]{1,0:T(8,128)S(1)} custom-call(f32[128,128]{1,0:T(8,128)S(1)} %convolution_subtract_fusion.2), custom_call_target="Cholesky" | custom-call | tf_op jit(solution)/shard_map/jit(cholesky)/cholesky | solution.py:55
  492.6 14.0 %while.1 = (s32[]{:T(128)}, f32[512,512]{1,0:T(8,128)}, s32[4,2]{0,1:T(2,128)S(1)}, f32[4,128,128]{2,1,0:T(8,128)}, s32[]{:T(128)}) while((s32[]{:T(128)}, f32[512,512]{1,0:T(8,128)}, s32[4,2]{0,1:T(2,128)S(1)}, f32[4,128,128]{2,1,0:T(8,128)}, s32[]{:T(128)}) %tuple.33), condition=%wide.while_cond, body=%wide.while_body.sunk | while | flops 2 | bytes 132705 | solution.py:56
  493.3 2.9 bitcast_dynamic-update-slice_fusion.2
  496.8 2.9 bitcast_dynamic-update-slice_fusion.2
  500.3 2.9 bitcast_dynamic-update-slice_fusion.2
  503.8 2.8 bitcast_dynamic-update-slice_fusion.2
  506.6 40.1 %custom-call.34 = f32[4,128,128]{1,2,0:T(8,128)S(1)} custom-call(f32[4,128,128]{2,1,0:T(8,128)} %get-tuple-element.10), custom_call_target="InvertDiagBlocksLowerTriangular" | custom-call | tf_op jit(solution)/shard_map/jit(_solve_triangular)/triangular_solve | solution.py:56
  551.9 40.7 %all-gather.4.cloned.1.call-done = f32[1024,512]{1,0:T(8,128)} async-done(((f32[64,512]{1,0:T(8,128)}), f32[1024,512]{1,0:T(8,128)}) %all-gather.4.cloned.1.call-update) | async-done | bytes 2097168 | tf_op jit(solution)/shard_map/all_gather | solution.py:57
  594.0 46.5 %collective-permute-done.2 = f32[1024,512]{1,0:T(8,128)S(1)} collective-permute-done((f32[1024,512]{1,0:T(8,128)}, f32[1024,512]{1,0:T(8,128)S(1)}, u32[]{:S(2)}, u32[]{:S(2)}) %collective-permute-start.2) | collective-permute-done | bytes 2097184 | tf_op jit(solution)/shard_map/ppermute | solution.py:12
  640.5 2.1 broadcast_select_fusion.2
  642.7 13.9 %fusion = f32[512,1024]{1,0:T(8,128)S(1)} fusion(f32[1024,512]{1,0:T(8,128)S(1)} %copy-done.1, f32[1,1,1024,1024]{3,2,1,0:T(8,128)S(1)} %copy-done.3), kind=kOutput, calls=%fused_computation.2 | convolution fusion | flops 6442450944 | bytes 8388608 | tf_op jit(solution)/shard_map/dot_general | solution.py:16
  656.6 7.7 %fusion.12 = f32[1,1,512,512]{3,2,1,0:T(8,128)} fusion(f32[512,1024]{1,0:T(8,128)S(1)} %fusion, f32[1024,512]{1,0:T(8,128)S(1)} %collective-permute-done.3, f32[1024,512]{1,0:T(8,128)S(1)} %broadcast_select_fusion.2, pred[]{:T(512)} %bitcast), kind=kOutput, calls=%fused_computation.14 | convolution fusion | flops 3221749760 | bytes 7340033 | tf_op jit(solution)/shard_map/rk,rl->kl/dot_general | solution.py:20
  (75 shorter events, 36.2 us)
Async XLA Ops:
  7.2 204.0 %copy-start = (f32[1024,512]{1,0:T(8,128)S(1)}, f32[1024,512]{1,0:T(8,128)}, u32[]{:S(2)}) copy-start(f32[1024,512]{1,0:T(8,128)} %param.8) | copy-start | bytes 6291460
  7.2 56.1 %all-gather.6.cloned.1.call-start = ((), (), s32[]{:S(2)}) async-start(), calls=%async_computation.2 | async-start | bytes 4456448 | tf_op jit(solution)/shard_map/all_gather | solution.py:28
  7.9 274.6 %reduce-scatter.4.cloned.1.call-start = ((), (), s32[]{:S(2)}) async-start(), calls=%async_computation.3 | async-start | bytes 4456448
  63.3 17.1 %copy-start.2 = (f32[1,1,1024,1024]{3,2,1,0:T(8,128)S(1)}, f32[1,1,1024,1024]{3,2,1,0:T(8,128)}, u32[]{:S(2)}) copy-start(f32[1,1,1024,1024]{3,2,1,0:T(8,128)} %param.5) | copy-start | bytes 12582916
  108.4 92.8 %collective-permute-start = (f32[1024,1024]{0,1:T(8,128)S(1)}, f32[1024,1024]{0,1:T(8,128)S(1)}, u32[]{:S(2)}, u32[]{:S(2)}) collective-permute-start(f32[1024,1024]{0,1:T(8,128)S(1)} %fusion.7), channel_id=1, source_target_pairs={{1,0},{0,1},{3,2},{2,3},{5,4},{4,5},{7,6},{6,7},{9,8},{8,9},{11,10... | collective-permute-start | bytes 12582920 | tf_op jit(solution)/shard_map/ppermute | solution.py:12
  202.5 0.3 collective-permute-start.1
  211.1 0.9 copy-start.5
  211.1 181.7 %all-reduce.6.cloned.1.call-start = ((), (), s32[]{:S(2)}) async-start(), calls=%async_computation.4 | async-start | bytes 6291456 | tf_op jit(solution)/shard_map/psum | solution.py:40
  282.6 6.7 copy-start.6
  289.0 303.5 %all-gather.4.cloned.1.call-start = ((), (), s32[]{:S(2)}) async-start(), calls=%async_computation.1 | async-start | bytes 2228224 | tf_op jit(solution)/shard_map/all_gather | solution.py:57
  400.8 1.0 copy-start.4
  592.5 50.2 %copy-start.1 = (f32[1024,512]{1,0:T(8,128)S(1)}, f32[1024,512]{1,0:T(8,128)}, u32[]{:S(2)}) copy-start(f32[1024,512]{1,0:T(8,128)} %all-gather.4.cloned.1.call-done) | copy-start | bytes 6291460
  592.5 50.2 %copy-start.3 = (f32[1,1,1024,1024]{3,2,1,0:T(8,128)S(1)}, f32[1,1,1024,1024]{3,2,1,0:T(8,128)}, u32[]{:S(2)}) copy-start(f32[1,1,1024,1024]{3,2,1,0:T(8,128)} %param.5) | copy-start | bytes 12582916
  592.5 48.0 %collective-permute-start.2 = (f32[1024,512]{1,0:T(8,128)}, f32[1024,512]{1,0:T(8,128)S(1)}, u32[]{:S(2)}, u32[]{:S(2)}) collective-permute-start(f32[1024,512]{1,0:T(8,128)} %all-gather.4.cloned.1.call-done), channel_id=1, source_target_pairs={{1,0},{0,1},{3,2},{2,3},{5,4},{4,5},{7,6},{6,7},{9,8},{8,9},{11,10... | collective-permute-start | bytes 6291464 | tf_op jit(solution)/shard_map/ppermute | solution.py:12
  642.6 14.0 %collective-permute-start.3 = (f32[1024,512]{1,0:T(8,128)S(1)}, f32[1024,512]{1,0:T(8,128)S(1)}, u32[]{:S(2)}, u32[]{:S(2)}) collective-permute-start(f32[1024,512]{1,0:T(8,128)S(1)} %broadcast_select_fusion.2), channel_id=1, source_target_pairs={{0,0},{1,1},{2,2},{3,3},{4,4},{5,5},{6,6},{7,7},{8,8},{9,9},{10,10... | collective-permute-start | bytes 6291464 | tf_op jit(solution)/shard_map/ppermute | solution.py:12
Sparse Core Ops, SparseCore 0:
  10.2 53.0 all-gather.5
  211.2 71.2 reduce-scatter.3
  289.1 103.6 all-reduce.5
  552.0 40.4 all-gather.3
where the time goes:
time: 678 us; the launch traced here: 672 us
  waiting for transfers between devices  363 us (54%)
  other arithmetic  135 us (20%)
  matrix products  86.2 us (13%)
  blocking collectives  36.9 us (5%)
  local copies, waits for them, and re-layouts  27 us (4%)
  between operations  19.9 us (3%)
    ppermute x4, waiting for transfers between devices, shifted_2(): return lax.ppermute(block, axis, route)  137 us
    another operation x14, other arithmetic, body(): factor = jnp.linalg.cholesky(gram_mat)  81 us
    unnamed x5, waiting for transfers between devices  67.9 us
    dot_general x5, matrix products, matmul(): jnp.dot(first, second, precision=EXACT, preferred_element_type=jnp.float32)  62.7 us
    psum x1, waiting for transfers between devices, body(): lax.psum((contract_rows(first_sk, first_sk), contract_rows(first_sk, seco...  62.5 us
    all_gather x1, waiting for transfers between devices, body(): lax.all_gather(state_slab, 'op', axis=0, tiled=True)  55.3 us
    another operation x3, other arithmetic, body(): jax.scipy.linalg.solve_triangular(factor, sketched.T, lower=True)  41.2 us
    all_gather x1, waiting for transfers between devices, body(): basis_full = lax.all_gather(basis_slab, 'op', axis=0, tiled=True)  40.7 us
  transfers between devices with their start and end apart: 8, of which 6 were waited for; matrix products, arithmetic and copies ran while one was open for 3% of the time, Pallas kernels for 0%

commit v1 on v0

v1 whole, which is shorter than its diff:
```python
import functools

import jax
import jax.numpy as jnp
from jax import lax
from jax.experimental import pallas as pl
from jax.experimental.pallas import tpu as pltpu
from jax.sharding import PartitionSpec as P

EXACT = lax.Precision.HIGHEST
SPLIT = lax.Precision.HIGH
HALF = 64
BLOCK = 128


def matmul(first, second, precision=SPLIT):
    return jnp.dot(first, second, precision=precision, preferred_element_type=jnp.float32)


def exact_nn(first, second):
    return lax.dot_general(first, second, (((1,), (0,)), ((), ())), precision=EXACT, preferred_element_type=jnp.float32)


def exact_nt(first, second):
    return lax.dot_general(first, second, (((1,), (1,)), ((), ())), precision=EXACT, preferred_element_type=jnp.float32)


def eliminate_many(blocks):
    sub = lax.broadcasted_iota(jnp.int32, (8, BLOCK), 0)
    lane = lax.broadcasted_iota(jnp.int32, (8, BLOCK), 1)
    rows = [[block[8 * c : 8 * c + 8, :] for c in range(HALF // 8)] for block in blocks]
    for j in range(HALF):
        home = j // 8
        for chunk in rows:
            row = chunk[home][j % 8 : j % 8 + 1, :]
            scaled = row / row[:, j : j + 1]
            for c in range(home, HALF // 8):
                column = jnp.broadcast_to(chunk[c][:, j : j + 1], (8, BLOCK))
                if c == home:
                    column = jnp.where(sub > j % 8, column, 0.0)
                chunk[c] = chunk[c] - column * scaled
    results = []
    for chunk in rows:
        scaled_chunks = []
        for c in range(HALF // 8):
            pivot = jnp.sum(jnp.where(lane == sub + 8 * c, chunk[c], 0.0), axis=1, keepdims=True)
            scaled_chunks.append(jnp.where(lane >= HALF, chunk[c] * lax.rsqrt(pivot), 0.0))
        results.append(jnp.concatenate(scaled_chunks, axis=0))
    return results


def invert_blocks(blocks):
    lane = lax.broadcasted_iota(jnp.int32, (HALF, BLOCK), 1)
    row = lax.broadcasted_iota(jnp.int32, (HALF, BLOCK), 0)
    unit = jnp.where(lane == row + HALF, 1.0, 0.0)
    empty = jnp.zeros((HALF, BLOCK), jnp.float32)

    def tall(top):
        return jnp.concatenate([top, empty], axis=0)

    first = eliminate_many([jnp.where(lane < HALF, block[:HALF], unit) for block in blocks])
    upper = [pltpu.roll(one, HALF, 1) for one in first]
    lower = [block[HALF:] for block in blocks]
    coupling = [exact_nt(low, tall(up)) for low, up in zip(lower, upper)]
    schur = [pltpu.roll(low, HALF, 1) - exact_nt(mid, tall(mid)) for low, mid in zip(lower, coupling)]
    second = eliminate_many([jnp.where(lane < HALF, one, unit) for one in schur])
    result = []
    for up, mid, right in zip(upper, coupling, second):
        carried = exact_nn(mid, tall(up))
        left = exact_nn(pltpu.roll(right, HALF, 1), tall(carried))
        result.append(jnp.concatenate([up, right - left], axis=0))
    return result


def inverse_factor_kernel(count, order, gram_ref, inverse_ref, work):
    row = lax.broadcasted_iota(jnp.int32, (order, order), 0)
    column = lax.broadcasted_iota(jnp.int32, (order, order), 1)
    for i in range(count):
        work[i] = gram_ref[i]
        inverse_ref[i] = jnp.where(row == column, 1.0, 0.0)
    tall_row = lax.broadcasted_iota(jnp.int32, (order, BLOCK), 0)

    def step(b, carry):
        start = pl.multiple_of(b * BLOCK, BLOCK)
        here = pl.ds(start, BLOCK)
        inverses = invert_blocks([work[i, here, here] for i in range(count)])
        for i in range(count):
            panel = jnp.where(tall_row >= start + BLOCK, work[i, :, here], 0.0)
            low = exact_nt(panel, inverses[i])
            strip = exact_nn(inverses[i], inverse_ref[i, here, :])
            inverse_ref[i] = inverse_ref[i] - exact_nn(low, strip)
            inverse_ref[i, here, :] = strip
            work[i] = work[i] - exact_nt(low, low)
        return carry

    lax.fori_loop(0, order // BLOCK, step, 0)


def inverse_factors(gram_pair):
    count, order, _ = gram_pair.shape
    return pl.pallas_call(
        functools.partial(inverse_factor_kernel, count, order),
        out_shape=jax.ShapeDtypeStruct(gram_pair.shape, jnp.float32),
        in_specs=[pl.BlockSpec(memory_space=pltpu.VMEM)],
        out_specs=pl.BlockSpec(memory_space=pltpu.VMEM),
        scratch_shapes=[pltpu.VMEM(gram_pair.shape, jnp.float32)],
        name="inverse_factors",
    )(gram_pair)


def body(left_ops, right_ops, amplitudes, sketch, sector_shift):
    left_op = left_ops[0, 0]
    right_op = right_ops[0, 0]
    state_slab = amplitudes[0]
    sectors = lax.axis_size("sec")
    slabs = lax.axis_size("op")
    height, width = state_slab.shape
    order = height * slabs
    keep = sketch.shape[1]
    source = lax.axis_index("sec")
    target = lax.rem(source + sector_shift[0], sectors)

    states = lax.all_gather(state_slab, ("sec", "op"), axis=0, tiled=True).reshape(sectors, order, width)
    right_sk = matmul(right_op, sketch)
    state_here = lax.dynamic_index_in_dim(states, source, 0, keepdims=False)
    term_sk = matmul(left_op, matmul(state_here, right_sk))
    mine = lax.broadcasted_iota(jnp.int32, (sectors, 1, 1), 0) == target
    spread = jnp.where(mine, term_sk[None], 0.0).reshape(sectors * order, keep)
    first_slab = lax.psum_scatter(spread, ("sec", "op"), scatter_dimension=0, tiled=True)

    state_there = lax.dynamic_index_in_dim(states, target, 0, keepdims=False)
    term_full = matmul(left_op, matmul(state_here, right_op))
    correlation = jnp.sum(state_there * term_full)
    norm_sq = jnp.sum(states * states)
    second_here = matmul(state_here, sketch)
    second_there = matmul(state_there, sketch)

    packed = jnp.concatenate([first_slab, jnp.full((8, keep), correlation, jnp.float32)], axis=0)
    gathered = lax.all_gather(packed, ("sec", "op"), axis=0, tiled=True).reshape(sectors, slabs, height + 8, keep)
    energy = jnp.sum(gathered[:, :, height, 0]) / norm_sq
    first_here = lax.dynamic_index_in_dim(gathered, source, 0, keepdims=False)[:, :height].reshape(order, keep)
    first_there = lax.dynamic_index_in_dim(gathered, target, 0, keepdims=False)[:, :height].reshape(order, keep)
    sketched = jnp.stack([first_here - energy * second_here, first_there - energy * second_there])
    gram_pair = jnp.einsum("srk,srl->skl", sketched, sketched, precision=EXACT)
    inverse_pair = inverse_factors(gram_pair)
    basis_here = lax.dot_general(sketched[0], inverse_pair[0], (((1,), (1,)), ((), ())), precision=SPLIT)
    basis_there = lax.dot_general(sketched[1], inverse_pair[1], (((1,), (1,)), ((), ())), precision=SPLIT)
    basis_slab = lax.dynamic_slice_in_dim(basis_here, lax.axis_index("op") * height, height, 0)
    applied = matmul(left_op, basis_here)
    rotated = jnp.einsum("rk,rl->kl", basis_there, applied, precision=SPLIT)
    return (rotated[None, None], basis_slab[None], energy)


def solution(mesh):
    in_specs = (
        P("op", "sec", None, None),
        P("op", "sec", None, None),
        P("sec", "op", None),
        P(),
        P("op"),
    )
    out_specs = (P("op", "sec", None, None), P("sec", "op", None), P())
    return jax.shard_map(body, mesh=mesh, in_specs=in_specs, out_specs=out_specs, check_vma=False)
```

time: 678 us -> 442 us (0.65)
  waiting for transfers between devices: 363 us -> 236 us
  other arithmetic: 135 us -> 11.6 us
  Pallas kernels: 0 us -> 67.1 us
  blocking collectives: 36.9 us -> 0 us
    ppermute x4 -> x0, waiting for transfers between devices: 137 us -> none  [shifted_2(): return lax.ppermute(block, axis, route)]
    another operation x17 -> x0, other arithmetic: 122 us -> none  [the longest x14 81 us: body(): factor = jnp.linalg.cholesky(gram_mat)]
    reduce_scatter x0 -> x1, waiting for transfers between devices: none -> 105 us  [body(): lax.psum_scatter(spread, ('sec', 'op'), scatter_dimension=0, tiled=True)]
    unnamed x5 -> x3, waiting for transfers between devices: 67.9 us -> 0.71 us
    pallas_call x0 -> x1, Pallas kernels: none -> 67.1 us  [inverse_factors(): pl.pallas_call(functools.partial(inverse_factor_kernel, count, order), ou...]
    psum x1 -> x0, waiting for transfers between devices: 62.5 us -> none  [body(): lax.psum((contract_rows(first_sk, first_sk), contract_rows(first_sk, seco...]
    psum x2 -> x0, blocking collectives: 36.9 us -> none  [the longest x1 30.9 us: body(): lax.psum((contract_rows(first_sk, first_sk), contract_rows(first_sk, seco...]
    all_gather x2, waiting for transfers between devices: 96 us -> 130 us  [the longest x1 74.9 us: body(): lax.all_gather(state_slab, ('sec', 'op'), axis=0, tiled=True)]
  transfers between devices with their start and end apart: 8 -> 3, of which waited for: 6 -> 3; matrix products, arithmetic and copies ran while one was open for 3% -> 11% of each run, Pallas kernels for 0% -> 0%
where the time goes in v1:
time: 442 us; the launch traced here: 438 us
  waiting for transfers between devices  236 us (53%)
  matrix products  82.3 us (19%)
  Pallas kernels  67.1 us (15%)
  local copies, waits for them, and re-layouts  24 us (5%)
  between operations  17.3 us (4%)
  other arithmetic  11.6 us (3%)
    reduce_scatter x1, waiting for transfers between devices, body(): lax.psum_scatter(spread, ('sec', 'op'), scatter_dimension=0, tiled=True)  105 us
    all_gather x1, waiting for transfers between devices, body(): lax.all_gather(state_slab, ('sec', 'op'), axis=0, tiled=True)  74.9 us
    pallas_call x1, Pallas kernels, inverse_factors(): pl.pallas_call(functools.partial(inverse_factor_kernel, count, order), ou...  67.1 us
    dot_general x8, matrix products, matmul(): jnp.dot(first, second, precision=precision, preferred_element_type=jnp.fl...  63.7 us
    all_gather x1, waiting for transfers between devices, body(): lax.all_gather(packed, ('sec', 'op'), axis=0, tiled=True)  55.4 us
  transfers between devices with their start and end apart: 3, of which 3 were waited for; matrix products, arithmetic and copies ran while one was open for 11% of the time, Pallas kernels for 0%

profile of v1, /device:TPU:0, one launch (start us, length us, event | category | flops | bytes accessed | tf_op | source)
XLA Modules:
  0.0 438.5 jit_solution(9551918437979840810)
XLA Ops:
  7.2 0.7 all-gather.6.cloned.1.call-update
  8.6 0.1 broadcast_in_dim.34
  8.8 7.0 %fusion.15 = f32[1024,512]{1,0:T(8,128)} fusion(f32[1024,512]{1,0:T(8,128)S(1)} %copy-done, f32[1,1,1024,1024]{3,2,1,0:T(8,128)} %param.6), kind=kOutput, calls=%fused_computation.18 | convolution fusion | flops 3221225472 | bytes 8388608 | tf_op jit(solution)/shard_map/dot_general | solution.py:17
  15.7 74.9 %all-gather.6.cloned.1.call-done = f32[1,2048,1024]{2,1,0:T(8,128)} async-done(((f32[1,64,1024]{2,1,0:T(8,128)}), f32[1,2048,1024]{2,1,0:T(8,128)}) %all-gather.6.cloned.1.call-update) | async-done | bytes 8388624 | tf_op jit(solution)/shard_map/all_gather | solution.py:123
  90.7 6.2 %fusion.20 = f32[1024,512]{1,0:T(8,128)S(1)} fusion(f32[1024,512]{1,0:T(8,128)} %fusion.15, f32[2,1024,1024]{2,1,0:T(8,128)} %bitcast.75, s32[]{:T(128)S(6)} %select_n.18), kind=kOutput, calls=%fused_computation.23 | convolution fusion | flops 3221225472 | bytes 8388612 | tf_op jit(solution)/shard_map/dot_general | solution.py:17
  96.9 8.2 %fusion.27 = f32[1024,512]{0,1:T(8,128)} fusion(f32[1024,512]{1,0:T(8,128)S(1)} %fusion.20, f32[1,1,1024,1024]{3,2,1,0:T(8,128)S(1)} %copy-done.2), kind=kOutput, calls=%fused_computation.32 | convolution fusion | flops 3221225472 | bytes 8388608 | tf_op jit(solution)/shard_map/dot_general | solution.py:17
  105.1 2.9 copy.8
  108.1 3.9 bitcast_select_fusion
  112.0 0.0 all-gather.4.cloned.1.call-start
  112.0 4.8 %constant_dynamic-slice_fusion = f32[1,1024,1024]{2,1,0:T(8,128)} fusion(f32[2,1024,1024]{2,1,0:T(8,128)} %bitcast.76, s32[]{:T(128)S(6)} %select_n.20), kind=kLoop, calls=%fused_computation.42 | loop fusion | bytes 8388612 | tf_op jit(solution)/shard_map/jit(dynamic_index_in_dim)/dynamic_slice | solution.py:131
  116.8 5.6 %copy.12 = f32[1,1024,1024]{1,2,0:T(8,128)} copy(f32[1,1024,1024]{2,1,0:T(8,128)} %constant_dynamic-slice_fusion) | data formatting | bytes 8388608
  122.4 10.6 %fusion.13 = f32[1024,1024]{1,0:T(8,128)S(1)} fusion(f32[1,1,1024,1024]{3,2,1,0:T(8,128)} %param.6, f32[2,1024,1024]{2,1,0:T(8,128)} %bitcast.77, s32[]{:T(128)S(6)} %select_n.18), kind=kOutput, calls=%fused_computation.16 | convolution fusion | flops 6442450944 | bytes 12582916 | tf_op jit(solution)/shard_map/dot_general | solution.py:17
  133.0 14.9 %fusion.6 = f32[]{:T(128)} fusion(f32[1,1024,1024]{1,2,0:T(8,128)S(1)} %copy-done.10, f32[1024,1024]{1,0:T(8,128)S(1)} %fusion.13, f32[1,1,1024,1024]{3,2,1,0:T(8,128)S(1)} %copy-done.3), kind=kOutput, calls=%fused_computation.8 | convolution fusion | flops 6444548096 | bytes 12582916 | tf_op jit(solution)/shard_map/dot_general | solution.py:17
  147.9 105.1 %reduce-scatter.2.cloned.1.call-done = f32[64,512]{1,0:T(8,128)} async-done(((f32[2048,512]{1,0:T(8,128)}), f32[64,512]{1,0:T(8,128)}) %reduce-scatter.2.cloned.1.call-update) | async-done | bytes 131088 | tf_op jit(solution)/shard_map/reduce_scatter | solution.py:129
  253.0 2.2 concatenate.3
  255.2 6.1 %multiply_reduce_fusion = f32[]{:T(128)} fusion(f32[1,2048,1024]{2,1,0:T(8,128)} %all-gather.6.cloned.1.call-done), kind=kLoop, calls=%fused_computation | loop fusion | flops 4194303 | bytes 8388612 | tf_op jit(solution)/shard_map/reduce_sum | solution.py:134
  261.4 55.4 %all-gather.4.cloned.1.call-done = f32[2304,512]{1,0:T(8,128)} async-done(((f32[72,512]{1,0:T(8,128)}), f32[2304,512]{1,0:T(8,128)}) %all-gather.4.cloned.1.call-update) | async-done | bytes 4718608 | tf_op jit(solution)/shard_map/all_gather | solution.py:139
  316.8 1.5 slice_reduce_fusion
  318.3 2.9 dynamic-slice_bitcast_fusion
  321.3 1.5 slice.22
  322.8 1.6 slice.20
  325.7 6.5 %bitcast_subtract_fusion = f32[1024,512]{1,0:T(8,128)S(1)} fusion(f32[16,64,512]{2,1,0:T(8,128)} %slice.22, f32[1024,512]{1,0:T(8,128)S(1)} %copy-done, f32[2,1024,1024]{2,1,0:T(8,128)} %bitcast.78, s32[]{:T(128)S(6)} %select_n.18, f32[]{:T(128)} %div.3), kind=kOutput, calls=%fused_computation.30 | convolution fusion | flops 3222274048 | bytes 10486276 | tf_op jit(solution)/shard_map/dot_general | solution.py:17
  332.2 3.5 bitcast_subtract_fusion.1
  335.7 1.3 copy-done.8
  337.1 8.3 %fusion.gram_ref = f32[2,512,512]{2,1,0:T(8,128)} fusion(f32[1,1024,512]{2,1,0:T(8,128)S(1)} %bitcast.80, f32[1,1024,512]{2,1,0:T(8,128)S(1)} %bitcast.79), kind=kOutput, calls=%fused_computation.1 | convolution fusion | flops 6443499520 | bytes 6291456 | tf_op jit(solution)/shard_map/srk,srl->skl/dot_general | solution.py:144
  345.4 67.1 %inverse_factors.1 = f32[2,512,512]{2,1,0:T(8,128)} custom-call(f32[2,512,512]{2,1,0:T(8,128)} %fusion.gram_ref), custom_call_target="tpu_custom_call" | custom-call | tf_op jit(solution)/shard_map/inverse_factors/pallas_call | solution.py:101
  412.5 3.9 fusion.34
  416.4 1.9 fusion.35
  418.3 0.3 copy-done.4
  418.6 6.8 %fusion.7 = f32[512,1024]{1,0:T(8,128)S(1)} fusion(f32[1024,512]{1,0:T(8,128)S(1)} %fusion.34, f32[1,1,1024,1024]{3,2,1,0:T(8,128)S(1)} %copy-done.4), kind=kOutput, calls=%fused_computation.10 | convolution fusion | flops 3221225472 | bytes 8388608 | tf_op jit(solution)/shard_map/dot_general | solution.py:17
  425.4 0.7 dynamic-slice_bitcast_fusion.2
  426.1 4.5 %convolution_bitcast_fusion = f32[1,1,512,512]{3,2,1,0:T(8,128)} fusion(f32[1024,512]{1,0:T(8,128)S(1)} %fusion.35, f32[512,1024]{1,0:T(8,128)S(1)} %fusion.7), kind=kOutput, calls=%fused_computation.33 | convolution fusion | flops 1610612736 | bytes 5242880 | tf_op jit(solution)/shard_map/rk,rl->kl/dot_general | solution.py:150
  (26 shorter events, 0.2 us)
Async XLA Ops:
  7.2 1.6 copy-start
  7.2 83.5 %all-gather.6.cloned.1.call-start = ((), (), s32[]{:S(2)}) async-start(), calls=%async_computation.3 | async-start | bytes 8650752 | tf_op jit(solution)/shard_map/all_gather | solution.py:123
  7.9 245.1 %reduce-scatter.2.cloned.1.call-start = ((), (), s32[]{:S(2)}) async-start(), calls=%async_computation.1 | async-start | bytes 4325376 | tf_op jit(solution)/shard_map/reduce_scatter | solution.py:129
  90.7 6.2 %copy-start.2 = (f32[1,1,1024,1024]{3,2,1,0:T(8,128)S(1)}, f32[1,1,1024,1024]{3,2,1,0:T(8,128)}, u32[]{:S(2)}) copy-start(f32[1,1,1024,1024]{3,2,1,0:T(8,128)} %param.5) | copy-start | bytes 12582916
  112.0 204.8 %all-gather.4.cloned.1.call-start = ((), (), s32[]{:S(2)}) async-start(), calls=%async_computation.2 | async-start | bytes 4866048 | tf_op jit(solution)/shard_map/all_gather | solution.py:139
  122.4 10.7 %copy-start.3 = (f32[1,1,1024,1024]{3,2,1,0:T(8,128)S(1)}, f32[1,1,1024,1024]{3,2,1,0:T(8,128)}, u32[]{:S(2)}) copy-start(f32[1,1,1024,1024]{3,2,1,0:T(8,128)} %param.5) | copy-start | bytes 12582916
  122.4 10.7 %copy-start.10 = (f32[1,1024,1024]{1,2,0:T(8,128)S(1)}, f32[1,1024,1024]{1,2,0:T(8,128)}, u32[]{:S(2)}) copy-start(f32[1,1024,1024]{1,2,0:T(8,128)} %copy.12) | copy-start | bytes 12582916
  325.7 6.5 %copy-start.1 = (f32[1,1024,1024]{2,1,0:T(8,128)S(1)}, f32[1,1024,1024]{2,1,0:T(8,128)}, u32[]{:S(2)}) copy-start(f32[1,1024,1024]{2,1,0:T(8,128)} %constant_dynamic-slice_fusion) | copy-start | bytes 12582916
  325.7 6.5 %copy-start.6 = (f32[16,64,512]{2,1,0:T(8,128)S(1)}, f32[16,64,512]{2,1,0:T(8,128)}, u32[]{:S(2)}) copy-start(f32[16,64,512]{2,1,0:T(8,128)} %slice.20) | copy-start | bytes 6291460
  332.2 3.5 copy-start.7
  335.7 1.3 copy-start.8
  412.5 3.9 copy-start.5
  412.5 3.9 copy-start.9
  416.4 2.2 copy-start.4
Sparse Core Ops, SparseCore 0:
  10.8 79.7 all-gather.5
  112.1 140.8 reduce-scatter.1
  256.4 60.3 all-gather.3
